TPU v7x, 128 devices: a whole 4x4x4 slice. The times are simulated.
128 devices in a mesh: leaf: 4 (over y), row: 8 (over z, core), col: 4 (over x).
Axes of the slice: x: 4, y: 4, z: 4, core: 2. Of those that a mesh axis runs over, the one named last changes fastest.
Arguments:
- sigma_top: float32 [1024, 1024], P(('leaf', 'row'), 'col')
- panels: float32 [4, 7, 1024, 512], P('leaf', None, 'row', 'col'), may hold values from -0.1875 to 0.1875
- inverse_diag: float32 [4, 7, 512, 512], P('leaf', None, 'col')
- slot_lists: int32 [4, 6, 8], P('leaf'), may hold values from -1 to 11, as said below
- parent_links: int32 [4, 4], P('leaf'), may hold values from 1 to 2
Outputs:
- ancestor_block: float32 [4, 7, 1024, 512], P('leaf', None, 'row', 'col')
- diagonal_block: float32 [4, 7, 512, 512], P('leaf', None, None, 'col')
Inputs may be any that keep to these rules, and one draw needn't show every extreme that they name: `slot_lists`: in every row, entries 0 to 3 are 8 to 11 in order (the parent's own tiles); then come 1 to 3 distinct parent ancestor slots, below 8 for supernodes 1 and 2 and below 4 for supernodes 3 to 6; the rest are -1, so every row has padding. `parent_links`: each supernode 3 to 6 has supernode 1 or 2 as its parent. `sigma_top`: symmetric.
All inputs are finite; a program needn't handle non-finite values.
Results may differ from a plain program's by a relative error of at most 0.0001.
Values sent between devices are 32-bit elements; how exact they have to be, the bound alone decides.
A program may use at most 128 MiB of HBM per device.

v0:
```python
import jax
import jax.numpy as jnp
from jax import lax
from jax.sharding import PartitionSpec as P

TILE = 128
HIGHEST = lax.Precision.HIGHEST


def mm(a, b):
    return jnp.matmul(a, b, precision=HIGHEST, preferred_element_type=jnp.float32)


def tile_rows(matrix, index, tile):
    return lax.dynamic_slice_in_dim(matrix, index * tile, tile, 0)


def tile_cols(matrix, index, tile):
    return lax.dynamic_slice_in_dim(matrix, index * tile, tile, 1)


def scatter_factor(factor_col, slots, positions, tile):
    tiles = factor_col.reshape(slots.shape[0], tile, factor_col.shape[1])
    hits = slots[:, None] == jnp.arange(positions, dtype=slots.dtype)[None, :]
    present = jnp.any(hits, axis=0)
    source = jnp.argmax(hits, axis=0)
    moved = jnp.take(tiles, source, axis=0)
    moved = jnp.where(present[:, None, None], moved, 0.0)
    return moved.reshape(positions * tile, factor_col.shape[1])


def pick_transposed(column_block, picks, tile):
    tiles = column_block.reshape(-1, tile, tile)
    chosen = jnp.take(tiles, jnp.maximum(picks, 0), axis=0)
    chosen = jnp.where((picks >= 0)[:, None, None], chosen, 0.0)
    return jnp.transpose(chosen, (2, 0, 1)).reshape(tile, picks.shape[0] * tile)


def body(sigma_top, panels, inverse_diag, slot_lists, parent_links):
    tile = TILE
    row_count = lax.axis_size("row")
    col_count = lax.axis_size("col")
    leaf_count = lax.axis_size("leaf")
    r = lax.axis_index("row")
    c = lax.axis_index("col")
    panel = panels[0]
    inverse = inverse_diag[0]
    picks_all = slot_lists[0]
    parents = parent_links[0]
    nodes = panel.shape[0]
    width = inverse.shape[2]
    own_tiles = width // tile
    slot_count = picks_all.shape[1]
    positions = slot_count + own_tiles
    band = width // row_count
    partial_factor = mm(panel, inverse)
    factor_rows = lax.psum(partial_factor, "col")
    living = jnp.concatenate([jnp.ones((1, slot_count), jnp.bool_), picks_all >= 0], axis=0)
    live_here = jnp.take(living, r, axis=1).astype(jnp.float32)
    factor_rows = factor_rows * live_here[:, None, None]
    factor_tile = lax.dynamic_slice_in_dim(factor_rows, c * tile, tile, 2)
    factor_cols = lax.all_gather(factor_tile, "row", axis=1, tiled=True)
    inverse_band = lax.dynamic_slice_in_dim(inverse, r * band, band, 2)
    partial_gram = mm(jnp.transpose(inverse_band, (0, 2, 1)), inverse)
    gram_piece = lax.psum_scatter(partial_gram, "col", scatter_dimension=2, tiled=True)
    local_rows, local_cols = sigma_top.shape
    gathered = lax.all_gather(sigma_top, ("leaf", "row", "col"), axis=0)
    sigma = gathered.reshape(leaf_count * row_count, col_count, local_rows, local_cols)
    sigma = jnp.transpose(sigma, (0, 2, 1, 3)).reshape(
        leaf_count * row_count * local_rows, col_count * local_cols
    )

    def diag_partial(first, products):
        rows = factor_rows[first : first + products.shape[0]]
        return mm(jnp.transpose(rows, (0, 2, 1)), products)

    def reduce_and_gather(first, products):
        count = products.shape[0]
        piece = lax.psum_scatter(
            diag_partial(first, products), "row", scatter_dimension=1, tiled=True
        )
        piece = piece + gram_piece[first : first + count]
        both = jnp.concatenate([products, piece], axis=1)
        everything = lax.all_gather(both, ("row", "col"), axis=0)
        everything = everything.reshape(row_count, col_count, count, tile + band, tile)
        product_full = jnp.transpose(everything[:, :, :, :tile], (2, 0, 3, 1, 4)).reshape(
            count, row_count * tile, col_count * tile
        )
        diag_full = jnp.transpose(everything[:, :, :, tile:], (2, 0, 3, 1, 4)).reshape(
            count, row_count * band, col_count * tile
        )
        return (product_full, diag_full)

    own_row = jnp.minimum(r, own_tiles - 1)
    upper = r < own_tiles
    product_0 = mm(tile_rows(sigma, r, tile), factor_cols[0])
    product_full_0, diag_full_0 = reduce_and_gather(0, product_0[None])
    product_full_0 = product_full_0[0]
    diag_full_0 = diag_full_0[0]
    level_1 = []
    for node in (1, 2):
        slots = picks_all[node - 1]
        spread = scatter_factor(factor_cols[node], slots, positions, tile)
        top_row = jnp.concatenate(
            [
                -jnp.transpose(tile_cols(product_full_0, own_row, tile)),
                tile_rows(diag_full_0, own_row, tile),
            ],
            axis=1,
        )
        source = slots[jnp.maximum(r, own_tiles)]
        source_row = jnp.maximum(source, 0)
        low_row = jnp.concatenate(
            [tile_rows(sigma, source_row, tile), -tile_rows(product_full_0, source_row, tile)],
            axis=1,
        )
        low_row = jnp.where(source >= 0, low_row, 0.0)
        row = jnp.where(upper, top_row, low_row)
        level_1.append(mm(row, spread))
    product_1 = jnp.stack(level_1)
    product_full_1, diag_full_1 = reduce_and_gather(1, product_1)
    level_2 = []
    for node in range(3, nodes):
        slots = picks_all[node - 1]
        parent = parents[node - 3] - 1
        parent_slots = jnp.take(picks_all, parent, axis=0)
        product_p = jnp.take(product_full_1, parent, axis=0)
        diag_p = jnp.take(diag_full_1, parent, axis=0)
        spread = scatter_factor(factor_cols[node], slots, positions, tile)
        top_row = jnp.concatenate(
            [-jnp.transpose(tile_cols(product_p, own_row, tile)), tile_rows(diag_p, own_row, tile)],
            axis=1,
        )
        source = slots[jnp.maximum(r, own_tiles)]
        source_row = jnp.clip(source, 0, own_tiles - 1)
        corner = pick_transposed(
            -tile_cols(product_full_0, source_row, tile), parent_slots[own_tiles:], tile
        )
        low_row = jnp.concatenate(
            [
                tile_rows(diag_full_0, source_row, tile),
                corner,
                -tile_rows(product_p, source_row, tile),
            ],
            axis=1,
        )
        low_row = jnp.where(source >= 0, low_row, 0.0)
        row = jnp.where(upper, top_row, low_row)
        level_2.append(mm(row, spread))
    product_2 = jnp.stack(level_2)
    first_2 = 3
    count_2 = product_2.shape[0]
    gram_rows = jnp.zeros((count_2, width, tile), jnp.float32)
    gram_rows = lax.dynamic_update_slice_in_dim(
        gram_rows, gram_piece[first_2 : first_2 + count_2], r * band, 1
    )
    diag_2 = lax.psum(diag_partial(first_2, product_2) + gram_rows, "row")
    products = jnp.concatenate([product_0[None], product_1, product_2], axis=0)
    diag_cols = jnp.concatenate(
        [
            tile_cols(diag_full_0, c, tile)[None],
            lax.dynamic_slice_in_dim(diag_full_1, c * tile, tile, 2),
            diag_2,
        ],
        axis=0,
    )
    return ((-products)[None], diag_cols[None])


def solution(mesh):
    return jax.shard_map(
        body,
        mesh=mesh,
        in_specs=(
            P(("leaf", "row"), "col"),
            P("leaf", None, "row", "col"),
            P("leaf", None, "col", None),
            P("leaf", None, None),
            P("leaf", None),
        ),
        out_specs=(P("leaf", None, "row", "col"), P("leaf", None, None, "col")),
        check_vma=False,
    )
```

profile of v0, /device:TPU:0, one launch (start us, length us, event | category | flops | bytes accessed | tf_op | source)
XLA Modules:
  0.0 459.2 jit_solution(14943117877159287603)
XLA Ops:
  8.1 1.4 copy-done
  9.5 3.9 fusion.2
  14.3 57.6 %all-reduce.4.cloned.1.call-done = f32[7,128,512]{2,1,0:T(8,128)} async-done(((f32[7,128,512]{2,1,0:T(8,128)}), f32[7,128,512]{2,1,0:T(8,128)}) %all-reduce.4.cloned.1.call-update) | async-done | bytes 1835024 | tf_op jit(solution)/shard_map/psum | solution.py:57
  72.0 1.8 broadcast_multiply_fusion
  73.7 1.2 copy-done.2
  75.9 2.3 fusion
  78.3 18.1 %all-gather.10.cloned.1.call-done = f32[4096,256]{1,0:T(8,128)} async-done(((f32[32,256]{1,0:T(8,128)}), f32[4096,256]{1,0:T(8,128)}) %all-gather.10.cloned.1.call-update) | async-done | bytes 4194320 | tf_op jit(solution)/shard_map/all_gather | solution.py:67
  96.3 5.8 %copy.83 = f32[32,4,32,256]{3,1,2,0:T(4,128)S(1)} copy(f32[32,4,32,256]{3,2,1,0:T(8,128)} %bitcast.194) | data formatting | bytes 8388608 | tf_op jit(solution)/shard_map/reshape | solution.py:68
  102.2 3.0 copy.124
  105.1 20.2 %all-gather.8.cloned.1.call-done = f32[7,1024,128]{2,1,0:T(8,128)} async-done(((f32[7,128,128]{2,1,0:T(8,128)}), f32[7,1024,128]{2,1,0:T(8,128)}) %all-gather.8.cloned.1.call-update) | async-done | bytes 3670032 | tf_op jit(solution)/shard_map/all_gather | solution.py:62
  125.3 2.5 bitcast_dynamic-update-slice_fusion.6
  127.8 1.3 convolution_bitcast_fusion
  129.2 30.5 %reduce-scatter.4.cloned.1.call-done = f32[1,64,128]{2,1,0:T(8,128)} async-done(((f32[1,512,128]{2,1,0:T(8,128)}), f32[1,64,128]{2,1,0:T(8,128)}) %reduce-scatter.4.cloned.1.call-update) | async-done | bytes 32784 | tf_op jit(solution)/shard_map/reduce_scatter | solution.py:79
  170.4 3.1 fusion.102
  173.5 1.5 gather_fusion.1
  175.0 1.5 gather_fusion
  176.4 2.3 select_select_fusion.4
  179.7 2.3 constant_dynamic-slice_fusion.22
  182.0 23.9 %all-gather.12.cloned.1.call-done = f32[32,192,128]{2,1,0:T(8,128)} async-done(((f32[1,192,128]{2,1,0:T(8,128)}), f32[32,192,128]{2,1,0:T(8,128)}) %all-gather.12.cloned.1.call-update) | async-done | bytes 3145744 | tf_op jit(solution)/shard_map/all_gather | solution.py:84
  206.0 1.3 slice.190
  207.3 3.2 slice.189
  210.5 2.9 copy.114
  213.3 2.1 copy.133
  217.1 1.4 dynamic-slice_negate_fusion
  219.5 1.8 copy.117
  221.3 1.7 neg.74
  224.9 2.9 bitcast_dynamic-update-slice_fusion.5
  227.8 1.6 bitcast_dynamic-update-slice_fusion.4
  229.4 1.8 fusion.71
  231.2 30.5 %reduce-scatter.8.cloned.1.call-done = f32[2,64,128]{2,1,0:T(8,128)} async-done(((f32[2,512,128]{2,1,0:T(8,128)}), f32[2,64,128]{2,1,0:T(8,128)}) %reduce-scatter.8.cloned.1.call-update) | async-done | bytes 65552 | tf_op jit(solution)/shard_map/reduce_scatter | solution.py:79
  270.7 1.3 iota_reduce_fusion.3
  271.9 1.2 iota_reduce_fusion.2
  274.2 2.5 gather_fusion.7
  276.8 1.5 gather_fusion.9
  278.3 1.5 gather_fusion.5
  280.4 2.3 select_select_fusion.1
  285.9 1.9 copy.123
  287.8 2.1 copy.108
  290.8 1.7 gather_fusion.6
  293.7 1.3 gather_fusion.4
  299.2 12.6 %all-gather.14.cloned.1.call-done = f32[64,192,128]{2,1,0:T(8,128)} async-done(((f32[2,192,128]{2,1,0:T(8,128)}), f32[64,192,128]{2,1,0:T(8,128)}) %all-gather.14.cloned.1.call-update) | async-done | bytes 6291472 | tf_op jit(solution)/shard_map/all_gather | solution.py:84
  311.9 3.2 slice.195
  315.0 4.7 %slice.194 = f32[8,4,2,128,128]{4,3,2,1,0:T(8,128)} slice(f32[8,4,2,192,128]{4,3,2,1,0:T(8,128)} %bitcast.193), slice={[0:8], [0:4], [0:2], [0:128], [0:128]} | slice | bytes 8388608 | tf_op jit(solution)/shard_map/slice | solution.py:86
  319.8 5.3 %copy.118 = f32[8,4,2,128,128]{3,0,4,1,2:T(8,128)} copy(f32[8,4,2,128,128]{4,3,2,1,0:T(8,128)} %slice.194) | data formatting | bytes 8388608
  325.0 4.9 %reshape.293 = f32[2,1024,512]{1,2,0:T(8,128)} reshape(f32[2,8,128,4,128]{2,1,4,3,0:T(8,128)} %bitcast.183) | data formatting | bytes 8388608 | tf_op jit(solution)/shard_map/reshape | solution.py:86
  329.9 4.3 copy.134
  334.2 3.1 reshape.294
  337.3 4.2 select_bitcast_fusion.4
  345.8 7.9 %select_bitcast_fusion = (f32[1024,512]{0,1:T(8,128)}, f32[1,1024,512]{1,2,0:T(8,128)}, f32[1,1024,512]{1,2,0:T(8,128)}, f32[1,1024,512]{1,2,0:T(8,128)}) fusion(f32[2,1024,512]{1,2,0:T(8,128)} %reshape.293, s32[]{:T(128)S(6)} %select_n.346, pred[]{:T(512)S(6)} %and.78, s32[]{:T(128)S(6)} %select_n.326, s32[]{:T(128)S(6)} %select_n.316, s32[]{:T(128)S(6)} %select_n.336), kind=kLoop, calls=%fused_computation.12 | loop fusion | flops 524288 | bytes 16777232 | tf_op jit(solution)/shard_map/jit(_take)/select_n | solution.py:127
  353.6 2.9 copy.121
  356.6 1.9 select_bitcast_fusion.2
  360.5 1.9 negate_bitcast_fusion
  363.7 3.0 copy.119
  366.7 1.9 select_bitcast_fusion.3
  370.6 2.9 copy.122
  373.5 1.9 select_bitcast_fusion.1
  377.5 3.3 bitcast_dynamic-update-slice_fusion.3
  380.8 1.6 bitcast_dynamic-update-slice_fusion.2
  382.4 1.6 bitcast_dynamic-update-slice_fusion.1
  384.0 1.6 bitcast_dynamic-update-slice_fusion
  385.6 1.8 fusion.62
  390.2 1.2 constant_dynamic-slice_fusion.8
  391.4 57.6 %all-reduce.6.cloned.1.call-done = f32[4,512,128]{2,1,0:T(8,128)} async-done(((f32[4,512,128]{2,1,0:T(8,128)}), f32[4,512,128]{2,1,0:T(8,128)}) %all-reduce.6.cloned.1.call-update) | async-done | bytes 1048592 | tf_op jit(solution)/shard_map/psum | solution.py:157
  449.1 2.6 maximum_bitcast_fusion
  (185 shorter events, 42.8 us)
Async XLA Ops:
  8.0 1.5 copy-start
  8.0 6.0 %copy-start.37 = (s32[1,6,8]{2,0,1:T(1,128)S(1)}, s32[1,6,8]{2,0,1:T(1,128)}, u32[]{:S(2)}) copy-start(s32[1,6,8]{2,0,1:T(1,128)} %param.18) | copy-start | bytes 580
  8.0 63.9 %all-reduce.4.cloned.1.call-start = ((), (), s32[]{:S(2)}) async-start(), calls=%async_computation.3 | async-start | bytes 3670016 | tf_op jit(solution)/shard_map/psum | solution.py:57
  13.4 82.9 %all-gather.10.cloned.1.call-start = ((), (), s32[]{:S(2)}) async-start(), calls=%async_computation.9 | async-start | bytes 4227072 | tf_op jit(solution)/shard_map/all_gather | solution.py:67
  14.0 111.3 %all-gather.8.cloned.1.call-start = ((), (), s32[]{:S(2)}) async-start(), calls=%async_computation.4 | async-start | bytes 4128768 | tf_op jit(solution)/shard_map/all_gather | solution.py:62
  73.7 1.2 copy-start.2
  75.8 53.4 %reduce-scatter.6.cloned.1.call-start = ((), (), s32[]{:S(2)}) async-start(), calls=%async_computation.6 | async-start | bytes 1146880 | tf_op jit(solution)/shard_map/reduce_scatter | solution.py:65
  78.2 81.5 %reduce-scatter.4.cloned.1.call-start = ((), (), s32[]{:S(2)}) async-start(), calls=%async_computation.5 | async-start | bytes 294912 | tf_op jit(solution)/shard_map/reduce_scatter | solution.py:79
  102.1 25.6 %copy-start.3 = (f32[7,128,512]{2,1,0:T(8,128)S(1)}, f32[7,128,512]{2,1,0:T(8,128)}, u32[]{:S(2)}) copy-start(f32[7,128,512]{2,1,0:T(8,128)} %copy-done.2) | copy-start | bytes 5505028
  129.1 76.9 %all-gather.12.cloned.1.call-start = ((), (), s32[]{:S(2)}) async-start(), calls=%async_computation.10 | async-start | bytes 3244032 | tf_op jit(solution)/shard_map/all_gather | solution.py:84
  161.2 100.5 %reduce-scatter.8.cloned.1.call-start = ((), (), s32[]{:S(2)}) async-start(), calls=%async_computation.7 | async-start | bytes 589824 | tf_op jit(solution)/shard_map/reduce_scatter | solution.py:79
  176.4 2.3 copy-start.12
  216.2 2.3 copy-start.5
  223.8 4.0 copy-start.16
  223.8 4.0 copy-start.21
  223.8 4.0 copy-start.30
  229.4 34.2 %copy-start.38 = (s32[1,4]{1,0:T(1,128)S(1)}, s32[1,4]{1,0:T(1,128)}, u32[]{:S(2)}) copy-start(s32[1,4]{1,0:T(1,128)} %param.19) | copy-start | bytes 52
  229.4 47.4 %copy-start.7 = (f32[1,1024,128]{2,1,0:T(8,128)S(1)}, f32[1,1024,128]{2,1,0:T(8,128)}, u32[]{:S(2)}) copy-start(f32[1,1024,128]{2,1,0:T(8,128)} %get-tuple-element.69) | copy-start | bytes 1572868
  231.2 47.1 %copy-start.6 = (f32[1,1024,128]{2,1,0:T(8,128)S(1)}, f32[1,1024,128]{2,1,0:T(8,128)}, u32[]{:S(2)}) copy-start(f32[1,1024,128]{2,1,0:T(8,128)} %get-tuple-element.71) | copy-start | bytes 1572868
  231.2 80.7 %all-gather.14.cloned.1.call-start = ((), (), s32[]{:S(2)}) async-start(), calls=%async_computation.11 | async-start | bytes 6488064 | tf_op jit(solution)/shard_map/all_gather | solution.py:84
  263.3 185.8 %all-reduce.6.cloned.1.call-start = ((), (), s32[]{:S(2)}) async-start(), calls=%async_computation.8 | async-start | bytes 2097152 | tf_op jit(solution)/shard_map/psum | solution.py:157
  280.4 2.3 copy-start.11
  280.4 3.4 copy-start.10
  283.8 6.0 %copy-start.19 = (f32[1024,128]{0,1:T(8,128)S(1)}, f32[1024,128]{0,1:T(8,128)}, u32[]{:S(2)}) copy-start(f32[1024,128]{0,1:T(8,128)} %get-tuple-element.76) | copy-start | bytes 1572868
  285.9 7.6 %copy-start.18 = (f32[1024,128]{0,1:T(8,128)S(1)}, f32[1024,128]{0,1:T(8,128)}, u32[]{:S(2)}) copy-start(f32[1024,128]{0,1:T(8,128)} %get-tuple-element.77) | copy-start | bytes 1572868
  290.8 6.0 %copy-start.17 = (f32[1024,128]{0,1:T(8,128)S(1)}, f32[1024,128]{0,1:T(8,128)}, u32[]{:S(2)}) copy-start(f32[1024,128]{0,1:T(8,128)} %get-tuple-element.78) | copy-start | bytes 1572868
  293.7 4.9 %copy-start.22 = (f32[1024,128]{1,0:T(8,128)S(1)}, f32[1024,128]{1,0:T(8,128)}, u32[]{:S(2)}) copy-start(f32[1024,128]{1,0:T(8,128)} %copy.108) | copy-start | bytes 1572868
  356.6 2.7 copy-start.34
  359.3 4.1 copy-start.31
  366.7 2.7 copy-start.33
  373.5 2.7 copy-start.32
  377.4 3.4 copy-start.8
  377.4 3.4 copy-start.15
  377.4 3.4 copy-start.24
  377.4 3.4 copy-start.26
  377.4 3.4 copy-start.29
  377.4 5.0 %copy-start.9 = (f32[128,1536]{1,0:T(8,128)S(1)}, f32[128,1536]{1,0:T(8,128)}, u32[]{:S(2)}) copy-start(f32[128,1536]{1,0:T(8,128)} %copy.106) | copy-start | bytes 2359300
  377.4 5.0 %copy-start.14 = (f32[12,128,128]{2,1,0:T(8,128)S(1)}, f32[12,128,128]{2,1,0:T(8,128)}, u32[]{:S(2)}) copy-start(f32[12,128,128]{2,1,0:T(8,128)} %select_select_fusion.1) | copy-start | bytes 2359300
  377.4 5.0 %copy-start.23 = (f32[128,512]{1,0:T(8,128)S(1)}, f32[128,512]{1,0:T(8,128)}, u32[]{:S(2)}) copy-start(f32[128,512]{1,0:T(8,128)} %get-tuple-element.87) | copy-start | bytes 786436
  377.4 5.0 %copy-start.27 = (f32[128,512]{1,0:T(8,128)S(1)}, f32[128,512]{1,0:T(8,128)}, u32[]{:S(2)}) copy-start(f32[128,512]{1,0:T(8,128)} %dynamic-slice_negate_fusion.5) | copy-start | bytes 786436
  377.4 5.0 %copy-start.28 = (f32[128,512]{1,0:T(8,128)S(1)}, f32[128,512]{1,0:T(8,128)}, u32[]{:S(2)}) copy-start(f32[128,512]{1,0:T(8,128)} %copy.105) | copy-start | bytes 786436
  380.8 3.2 copy-start.13
  380.8 3.2 copy-start.20
  380.8 3.2 copy-start.25
  385.6 1.8 copy-start.36
  387.4 2.0 copy-start.35
  387.4 1.0 copy-start.4
  390.2 61.4 %copy-start.1 = (f32[1,7,128,512]{3,2,1,0:T(8,128)S(1)}, f32[1,7,128,512]{3,2,1,0:T(8,128)}, u32[]{:S(2)}) copy-start(f32[1,7,128,512]{3,2,1,0:T(8,128)} %param.17) | copy-start | bytes 5505028
Sparse Core Ops, SparseCore 0:
  13.5 58.3 all-reduce.3
  79.1 22.6 reduce-scatter.5
  129.2 30.4 reduce-scatter.3
  162.1 43.8 all-gather.11
  231.3 30.3 reduce-scatter.7
  263.8 48.0 all-gather.13
Sparse Core Ops, SparseCore 1:
  17.0 79.3 all-gather.9
  98.5 26.8 all-gather.7
  388.5 60.5 all-reduce.5
where the time goes:
time: 461 us; the launch traced here: 459 us
  waiting for transfers between devices  252 us (55%)
  local copies, waits for them, and re-layouts  100 us (22%)
  other arithmetic  53.9 us (12%)
  between operations  26.5 us (6%)
  matrix products  26 us (6%)
    reduce_scatter x2, waiting for transfers between devices, reduce_and_gather(): lax.psum_scatter(diag_partial(first, products), 'row', scatter_dimension=...  61 us
    psum x1, waiting for transfers between devices, body(): factor_rows = lax.psum(partial_factor, 'col')  57.6 us
    psum x1, waiting for transfers between devices, body(): diag_2 = lax.psum(diag_partial(first_2, product_2) + gram_rows, 'row')  57.6 us
    all_gather x2, waiting for transfers between devices, reduce_and_gather(): everything = lax.all_gather(both, ('row', 'col'), axis=0)  36.5 us
    unnamed x92, local copies, waits for them, and re-layouts  35.4 us
    dot_general x12, matrix products, mm(): jnp.matmul(a, b, precision=HIGHEST, preferred_element_type=jnp.float32)  26 us
    all_gather x1, waiting for transfers between devices, body(): factor_cols = lax.all_gather(factor_tile, 'row', axis=1, tiled=True)  20.2 us
    all_gather x1, waiting for transfers between devices, body(): gathered = lax.all_gather(sigma_top, ('leaf', 'row', 'col'), axis=0)  18.1 us
  transfers between devices with their start and end apart: 9, of which 8 were waited for; matrix products, arithmetic and copies ran while one was open for 15% of the time, Pallas kernels for 0%

commit v1 on v0

--- a/solution.py
+++ b/solution.py
@@ -59,7 +59,13 @@
     live_here = jnp.take(living, r, axis=1).astype(jnp.float32)
     factor_rows = factor_rows * live_here[:, None, None]
     factor_tile = lax.dynamic_slice_in_dim(factor_rows, c * tile, tile, 2)
-    factor_cols = lax.all_gather(factor_tile, "row", axis=1, tiled=True)
+    expand_the_pages = lambda in_array, mesh_name: jnp.concatenate(
+        lax.all_to_all(
+            jnp.stack([in_array for _ in range(lax.axis_size(mesh_name))]), mesh_name, 0, 0
+        ),
+        axis=1,
+    )
+    factor_cols = expand_the_pages(factor_tile, "row")
     inverse_band = lax.dynamic_slice_in_dim(inverse, r * band, band, 2)
     partial_gram = mm(jnp.transpose(inverse_band, (0, 2, 1)), inverse)
     gram_piece = lax.psum_scatter(partial_gram, "col", scatter_dimension=2, tiled=True)

time: 461 us -> 474 us (1.028)
  waiting for transfers between devices: 252 us -> 260 us
    all_to_all x0 -> x1, waiting for transfers between devices: none -> 44.6 us  [body(): lax.all_to_all(jnp.stack([in_array for _ in range(lax.axis_size(mesh_name...]
    all_gather x1 -> x0, waiting for transfers between devices: 20.2 us -> none  [body(): factor_cols = lax.all_gather(factor_tile, 'row', axis=1, tiled=True)]
    all_gather x1, waiting for transfers between devices: 18.1 us -> 0.01 us  [body(): gathered = lax.all_gather(sigma_top, ('leaf', 'row', 'col'), axis=0)]
    another operation x0 -> x2, local copies, waits for them, and re-layouts: none -> 5.87 us  [the longest x1 3.48 us: scatter_factor(): tiles = factor_col.reshape(slots.shape[0], tile, factor_col.shape[1])]
    unnamed x92 -> x96, local copies, waits for them, and re-layouts: 35.4 us -> 35.4 us
  transfers between devices with their start and end apart: 9 -> 9, of which waited for: 8 -> 7; matrix products, arithmetic and copies ran while one was open for 15% -> 14% of each run, Pallas kernels for 0% -> 0%
where the time goes in v1:
time: 474 us; the launch traced here: 473 us
  waiting for transfers between devices  260 us (55%)
  local copies, waits for them, and re-layouts  102 us (22%)
  other arithmetic  53.7 us (11%)
  between operations  26.5 us (6%)
  matrix products  24.7 us (5%)
  starting transfers between devices  5.23 us (1%)
    reduce_scatter x2, waiting for transfers between devices, reduce_and_gather(): lax.psum_scatter(diag_partial(first, products), 'row', scatter_dimension=...  59.6 us
    psum x1, waiting for transfers between devices, body(): diag_2 = lax.psum(diag_partial(first_2, product_2) + gram_rows, 'row')  57.9 us
    psum x1, waiting for transfers between devices, body(): factor_rows = lax.psum(partial_factor, 'col')  57.7 us
    all_to_all x1, waiting for transfers between devices, body(): lax.all_to_all(jnp.stack([in_array for _ in range(lax.axis_size(mesh_name...  44.6 us
    all_gather x2, waiting for transfers between devices, reduce_and_gather(): everything = lax.all_gather(both, ('row', 'col'), axis=0)  39.8 us
    unnamed x96, local copies, waits for them, and re-layouts  35.4 us
    dot_general x12, matrix products, mm(): jnp.matmul(a, b, precision=HIGHEST, preferred_element_type=jnp.float32)  24.7 us
    select_n x4, other arithmetic, body(): product_p = jnp.take(product_full_1, parent, axis=0)  13.4 us
  transfers between devices with their start and end apart: 9, of which 7 were waited for; matrix products, arithmetic and copies ran while one was open for 14% of the time, Pallas kernels for 0%

profile of v1, /device:TPU:0, one launch (start us, length us, event | category | flops | bytes accessed | tf_op | source)
XLA Modules:
  0.0 472.5 jit_solution(10889573823009870715)
XLA Ops:
  8.1 1.4 copy-done
  9.5 3.9 fusion.2
  14.3 57.7 %all-reduce.4.cloned.1.call-done = f32[7,128,512]{2,1,0:T(8,128)} async-done(((f32[7,128,512]{2,1,0:T(8,128)}), f32[7,128,512]{2,1,0:T(8,128)}) %all-reduce.4.cloned.1.call-update) | async-done | bytes 1835024 | tf_op jit(solution)/shard_map/psum | solution.py:57
  72.0 1.8 broadcast_multiply_fusion
  73.7 1.2 copy-done.2
  75.0 2.4 stack.35
  77.4 4.5 all-to-all-start
  82.0 2.2 fusion
  84.3 44.6 %all-to-all-done = f32[8,7,128,128]{3,2,1,0:T(8,128)} async-done(((f32[8,7,128,128]{3,2,1,0:T(8,128)}), f32[8,7,128,128]{3,2,1,0:T(8,128)}, u32[]{:S(2)}, u32[]{:S(2)}) %all-to-all-start) | async-done | bytes 3670048 | tf_op jit(solution)/shard_map/all_to_all | solution.py:63
  128.8 3.5 slice_bitcast_fusion
  132.3 5.8 %copy.83 = f32[32,4,32,256]{3,1,2,0:T(4,128)S(1)} copy(f32[32,4,32,256]{3,2,1,0:T(8,128)} %bitcast.198) | data formatting | bytes 8388608 | tf_op jit(solution)/shard_map/reshape | solution.py:74
  139.2 1.9 copy-done.4
  141.1 1.3 bitcast_dynamic-update-slice_fusion.6
  142.3 1.3 convolution_bitcast_fusion
  143.7 29.1 %reduce-scatter.4.cloned.1.call-done = f32[1,64,128]{2,1,0:T(8,128)} async-done(((f32[1,512,128]{2,1,0:T(8,128)}), f32[1,64,128]{2,1,0:T(8,128)}) %reduce-scatter.4.cloned.1.call-update) | async-done | bytes 32784 | tf_op jit(solution)/shard_map/reduce_scatter | solution.py:85
  183.5 1.5 gather_fusion.1
  185.0 1.5 gather_fusion
  186.5 2.2 select_select_fusion.4
  189.7 2.3 constant_dynamic-slice_fusion.22
  192.0 27.2 %all-gather.9.cloned.1.call-done = f32[32,192,128]{2,1,0:T(8,128)} async-done(((f32[1,192,128]{2,1,0:T(8,128)}), f32[32,192,128]{2,1,0:T(8,128)}) %all-gather.9.cloned.1.call-update) | async-done | bytes 3145744 | tf_op jit(solution)/shard_map/all_gather | solution.py:90
  219.2 1.3 slice.197
  220.5 3.2 slice.196
  223.7 2.9 copy.114
  226.6 2.1 copy.133
  230.3 1.4 dynamic-slice_negate_fusion
  232.7 1.8 copy.117
  234.5 1.7 neg.74
  238.1 2.9 bitcast_dynamic-update-slice_fusion.5
  241.0 1.6 bitcast_dynamic-update-slice_fusion.4
  242.5 1.8 fusion.71
  244.4 30.5 %reduce-scatter.8.cloned.1.call-done = f32[2,64,128]{2,1,0:T(8,128)} async-done(((f32[2,512,128]{2,1,0:T(8,128)}), f32[2,64,128]{2,1,0:T(8,128)}) %reduce-scatter.8.cloned.1.call-update) | async-done | bytes 65552 | tf_op jit(solution)/shard_map/reduce_scatter | solution.py:85
  284.0 1.2 iota_reduce_fusion.3
  287.4 2.5 gather_fusion.9
  290.0 1.5 gather_fusion.7
  291.5 1.5 gather_fusion.5
  293.6 2.3 select_select_fusion
  299.1 1.9 copy.123
  301.0 2.0 copy.108
  304.0 1.7 gather_fusion.6
  306.8 1.3 gather_fusion.4
  312.4 12.7 %all-gather.11.cloned.1.call-done = f32[64,192,128]{2,1,0:T(8,128)} async-done(((f32[2,192,128]{2,1,0:T(8,128)}), f32[64,192,128]{2,1,0:T(8,128)}) %all-gather.11.cloned.1.call-update) | async-done | bytes 6291472 | tf_op jit(solution)/shard_map/all_gather | solution.py:90
  325.1 3.2 slice.202
  328.3 4.7 %slice.201 = f32[8,4,2,128,128]{4,3,2,1,0:T(8,128)} slice(f32[8,4,2,192,128]{4,3,2,1,0:T(8,128)} %bitcast.197), slice={[0:8], [0:4], [0:2], [0:128], [0:128]} | slice | bytes 8388608 | tf_op jit(solution)/shard_map/slice | solution.py:92
  333.0 5.3 %copy.118 = f32[8,4,2,128,128]{3,0,4,1,2:T(8,128)} copy(f32[8,4,2,128,128]{4,3,2,1,0:T(8,128)} %slice.201) | data formatting | bytes 8388608
  338.2 4.9 %reshape.314 = f32[2,1024,512]{1,2,0:T(8,128)} reshape(f32[2,8,128,4,128]{2,1,4,3,0:T(8,128)} %bitcast.187) | data formatting | bytes 8388608 | tf_op jit(solution)/shard_map/reshape | solution.py:92
  343.1 4.3 copy.134
  347.5 3.1 reshape.315
  350.6 4.2 select_bitcast_fusion.4
  359.0 7.9 %select_bitcast_fusion = (f32[1024,512]{0,1:T(8,128)}, f32[1,1024,512]{1,2,0:T(8,128)}, f32[1,1024,512]{1,2,0:T(8,128)}, f32[1,1024,512]{1,2,0:T(8,128)}) fusion(f32[2,1024,512]{1,2,0:T(8,128)} %reshape.314, s32[]{:T(128)S(6)} %select_n.346, pred[]{:T(512)S(6)} %and.78, s32[]{:T(128)S(6)} %select_n.326, s32[]{:T(128)S(6)} %select_n.316, s32[]{:T(128)S(6)} %select_n.336), kind=kLoop, calls=%fused_computation.12 | loop fusion | flops 524288 | bytes 16777232 | tf_op jit(solution)/shard_map/jit(_take)/select_n | solution.py:133
  366.8 2.9 copy.121
  369.8 1.9 select_bitcast_fusion.2
  373.7 1.9 negate_bitcast_fusion
  376.9 3.0 copy.119
  379.9 1.9 select_bitcast_fusion.3
  383.8 2.9 copy.122
  386.7 1.9 select_bitcast_fusion.1
  390.7 3.3 bitcast_dynamic-update-slice_fusion.3
  394.1 1.6 bitcast_dynamic-update-slice_fusion.2
  395.7 1.6 bitcast_dynamic-update-slice_fusion.1
  397.2 1.6 bitcast_dynamic-update-slice_fusion
  398.8 1.8 fusion.62
  403.4 1.2 constant_dynamic-slice_fusion.8
  404.7 57.9 %all-reduce.6.cloned.1.call-done = f32[4,512,128]{2,1,0:T(8,128)} async-done(((f32[4,512,128]{2,1,0:T(8,128)}), f32[4,512,128]{2,1,0:T(8,128)}) %all-reduce.6.cloned.1.call-update) | async-done | bytes 1048592 | tf_op jit(solution)/shard_map/psum | solution.py:163
  462.5 2.6 maximum_bitcast_fusion
  (189 shorter events, 44.1 us)
Async XLA Ops:
  8.0 1.5 copy-start
  8.0 6.0 %copy-start.39 = (s32[1,6,8]{2,0,1:T(1,128)S(1)}, s32[1,6,8]{2,0,1:T(1,128)}, u32[]{:S(2)}) copy-start(s32[1,6,8]{2,0,1:T(1,128)} %param.18) | copy-start | bytes 580
  8.0 63.9 %all-reduce.4.cloned.1.call-start = ((), (), s32[]{:S(2)}) async-start(), calls=%async_computation.4 | async-start | bytes 3670016 | tf_op jit(solution)/shard_map/psum | solution.py:57
  13.4 118.9 %all-gather.7.cloned.1.call-start = ((), (), s32[]{:S(2)}) async-start(), calls=%async_computation.9 | async-start | bytes 4227072 | tf_op jit(solution)/shard_map/all_gather | solution.py:73
  73.7 1.2 copy-start.2
  77.4 51.4 %all-to-all-start = ((f32[8,7,128,128]{3,2,1,0:T(8,128)}), f32[8,7,128,128]{3,2,1,0:T(8,128)}, u32[]{:S(2)}, u32[]{:S(2)}) async-start(f32[8,7,128,128]{3,2,1,0:T(8,128)} %stack.35), calls=%async_computation | async-start | bytes 7340032 | tf_op jit(solution)/shard_map/all_to_all | solution.py:63
  81.9 61.8 %reduce-scatter.6.cloned.1.call-start = ((), (), s32[]{:S(2)}) async-start(), calls=%async_computation.6 | async-start | bytes 1146880 | tf_op jit(solution)/shard_map/reduce_scatter | solution.py:71
  84.2 88.7 %reduce-scatter.4.cloned.1.call-start = ((), (), s32[]{:S(2)}) async-start(), calls=%async_computation.5 | async-start | bytes 294912 | tf_op jit(solution)/shard_map/reduce_scatter | solution.py:85
  138.1 3.0 copy-start.18
  138.1 4.3 copy-start.3
  139.1 1.9 copy-start.4
  143.7 75.5 %all-gather.9.cloned.1.call-start = ((), (), s32[]{:S(2)}) async-start(), calls=%async_computation.10 | async-start | bytes 3244032 | tf_op jit(solution)/shard_map/all_gather | solution.py:90
  174.3 100.5 %reduce-scatter.8.cloned.1.call-start = ((), (), s32[]{:S(2)}) async-start(), calls=%async_computation.7 | async-start | bytes 589824 | tf_op jit(solution)/shard_map/reduce_scatter | solution.py:85
  186.4 2.2 copy-start.13
  229.4 2.3 copy-start.6
  237.0 4.0 copy-start.17
  237.0 4.0 copy-start.23
  237.0 4.0 copy-start.32
  242.5 34.2 %copy-start.40 = (s32[1,4]{1,0:T(1,128)S(1)}, s32[1,4]{1,0:T(1,128)}, u32[]{:S(2)}) copy-start(s32[1,4]{1,0:T(1,128)} %param.19) | copy-start | bytes 52
  242.5 47.4 %copy-start.8 = (f32[8,128,128]{2,1,0:T(8,128)S(1)}, f32[8,128,128]{2,1,0:T(8,128)}, u32[]{:S(2)}) copy-start(f32[8,128,128]{2,1,0:T(8,128)} %get-tuple-element.70) | copy-start | bytes 1572868
  244.3 47.1 %copy-start.7 = (f32[8,128,128]{2,1,0:T(8,128)S(1)}, f32[8,128,128]{2,1,0:T(8,128)}, u32[]{:S(2)}) copy-start(f32[8,128,128]{2,1,0:T(8,128)} %get-tuple-element.71) | copy-start | bytes 1572868
  244.4 80.7 %all-gather.11.cloned.1.call-start = ((), (), s32[]{:S(2)}) async-start(), calls=%async_computation.11 | async-start | bytes 6488064 | tf_op jit(solution)/shard_map/all_gather | solution.py:90
  276.4 186.1 %all-reduce.6.cloned.1.call-start = ((), (), s32[]{:S(2)}) async-start(), calls=%async_computation.8 | async-start | bytes 2097152 | tf_op jit(solution)/shard_map/psum | solution.py:163
  293.6 2.3 copy-start.12
  293.6 3.4 copy-start.11
  297.0 6.0 %copy-start.21 = (f32[1024,128]{0,1:T(8,128)S(1)}, f32[1024,128]{0,1:T(8,128)}, u32[]{:S(2)}) copy-start(f32[1024,128]{0,1:T(8,128)} %get-tuple-element.77) | copy-start | bytes 1572868
  299.1 7.5 %copy-start.20 = (f32[1024,128]{0,1:T(8,128)S(1)}, f32[1024,128]{0,1:T(8,128)}, u32[]{:S(2)}) copy-start(f32[1024,128]{0,1:T(8,128)} %get-tuple-element.78) | copy-start | bytes 1572868
  304.0 6.0 %copy-start.19 = (f32[1024,128]{0,1:T(8,128)S(1)}, f32[1024,128]{0,1:T(8,128)}, u32[]{:S(2)}) copy-start(f32[1024,128]{0,1:T(8,128)} %get-tuple-element.79) | copy-start | bytes 1572868
  306.8 4.9 %copy-start.24 = (f32[1024,128]{1,0:T(8,128)S(1)}, f32[1024,128]{1,0:T(8,128)}, u32[]{:S(2)}) copy-start(f32[1024,128]{1,0:T(8,128)} %copy.108) | copy-start | bytes 1572868
  369.8 2.7 copy-start.36
  372.5 4.1 copy-start.33
  379.9 2.7 copy-start.35
  386.7 2.7 copy-start.34
  390.6 3.4 copy-start.9
  390.6 3.4 copy-start.16
  390.6 3.4 copy-start.26
  390.6 3.4 copy-start.28
  390.6 3.4 copy-start.31
  390.6 5.0 %copy-start.10 = (f32[128,1536]{1,0:T(8,128)S(1)}, f32[128,1536]{1,0:T(8,128)}, u32[]{:S(2)}) copy-start(f32[128,1536]{1,0:T(8,128)} %copy.106) | copy-start | bytes 2359300
  390.6 5.0 %copy-start.15 = (f32[12,128,128]{2,1,0:T(8,128)S(1)}, f32[12,128,128]{2,1,0:T(8,128)}, u32[]{:S(2)}) copy-start(f32[12,128,128]{2,1,0:T(8,128)} %select_select_fusion.1) | copy-start | bytes 2359300
  390.7 5.0 %copy-start.25 = (f32[128,512]{1,0:T(8,128)S(1)}, f32[128,512]{1,0:T(8,128)}, u32[]{:S(2)}) copy-start(f32[128,512]{1,0:T(8,128)} %get-tuple-element.88) | copy-start | bytes 786436
  390.7 5.0 %copy-start.29 = (f32[128,512]{1,0:T(8,128)S(1)}, f32[128,512]{1,0:T(8,128)}, u32[]{:S(2)}) copy-start(f32[128,512]{1,0:T(8,128)} %dynamic-slice_negate_fusion.5) | copy-start | bytes 786436
  390.7 5.0 %copy-start.30 = (f32[128,512]{1,0:T(8,128)S(1)}, f32[128,512]{1,0:T(8,128)}, u32[]{:S(2)}) copy-start(f32[128,512]{1,0:T(8,128)} %copy.105) | copy-start | bytes 786436
  394.0 3.2 copy-start.14
  394.1 3.2 copy-start.22
  394.1 3.2 copy-start.27
  398.8 1.8 copy-start.38
  400.6 2.0 copy-start.37
  400.7 1.0 copy-start.5
  403.4 61.7 %copy-start.1 = (f32[1,7,128,512]{3,2,1,0:T(8,128)S(1)}, f32[1,7,128,512]{3,2,1,0:T(8,128)}, u32[]{:S(2)}) copy-start(f32[1,7,128,512]{3,2,1,0:T(8,128)} %param.17) | copy-start | bytes 5505028
Sparse Core Ops, SparseCore 0:
  13.5 58.3 all-reduce.3
  85.2 23.0 reduce-scatter.5
  143.8 29.0 reduce-scatter.3
  175.2 43.8 all-gather.8
  244.5 30.3 reduce-scatter.7
  277.0 48.0 all-gather.10
  401.8 60.7 all-reduce.5
Sparse Core Ops, SparseCore 1:
  17.0 80.5 all-gather.6
